TPU v7x, 512 devices: a whole 4x8x8 slice. The times are simulated.
512 devices in a mesh: lat: 16 (over y, core), wave: 32 (over z, x).
Axes of the slice: x: 4, y: 8, z: 8, core: 2. Of those that a mesh axis runs over, the one named last changes fastest.
Arguments:
- fourier: bfloat16 [1024, 12, 1280], P(('lat', 'wave')), may hold values from -6 to 6
- wave_table: int32 [1280], replicated, may hold values from 0 to 1279, each once
- legendre: bfloat16 [1280, 512, 1280], P('wave', 'lat'), may hold values from -0.25 to 0.25
Outputs:
- spectral: float32 [1280, 12, 1280], P('wave', None, 'lat')
Inputs may be any that keep to these rules, and one draw needn't show every extreme that they name: `wave_table`: every wavenumber 0 to 1279 stands in exactly one slot.
All inputs are finite; a program needn't handle non-finite values.
Results may differ from a plain program's by a relative error of at most 0.0031.
Values may be sent and summed in bfloat16 or wider, within the bound.
A program may use at most 128 MiB of HBM per device.

v0:
```python
import jax
import jax.numpy as jnp
from jax import lax
from jax.sharding import PartitionSpec as P


def partner(block, axis, stride):
    count = lax.axis_size(axis)
    route = []
    for low in range(count):
        high = low | 1 << stride
        if high != low and high < count:
            route += [(low, high), (high, low)]
    return lax.ppermute(block, axis, route)


def local(fourier, wave_table, legendre):
    slot_count, pair_count, degree_count = legendre.shape
    lat_count = lax.axis_size("lat")
    half_degrees = degree_count // 2
    slice_width = degree_count // lat_count
    lat_index = lax.axis_index("lat")
    ordered = jnp.take(fourier, wave_table, axis=2)
    arrived = lax.all_to_all(ordered, "wave", split_axis=2, concat_axis=0, tiled=True)
    local_rows = jnp.transpose(arrived, (2, 1, 0))
    kept_rows = local_rows[:, :, :pair_count]
    received = local_rows[:, :, pair_count:]
    for bit_number in range(lat_count.bit_length() - 1):
        received = partner(received, "lat", bit_number)
    northern = lat_index < lat_count // 2
    north_rows = jnp.where(northern, kept_rows, received).astype(jnp.float32)
    south_rows = jnp.where(northern, jnp.flip(received, 2), jnp.flip(kept_rows, 2)).astype(
        jnp.float32
    )
    even_part = (north_rows + south_rows).astype(jnp.bfloat16)
    odd_part = (north_rows - south_rows).astype(jnp.bfloat16)
    my_waves = lax.dynamic_slice_in_dim(wave_table, lax.axis_index("wave") * slot_count, slot_count)
    even_out = jnp.einsum(
        "mcp,mpk->mck", even_part, legendre[:, :, :half_degrees], preferred_element_type=jnp.float32
    )
    odd_out = jnp.einsum(
        "mcp,mpk->mck", odd_part, legendre[:, :, half_degrees:], preferred_element_type=jnp.float32
    )
    partial_terms = jnp.concatenate([even_out, odd_out], axis=2)
    spectral = lax.psum_scatter(partial_terms, "lat", scatter_dimension=2, tiled=True)
    degree_slot = lat_index * slice_width + jnp.arange(slice_width, dtype=jnp.int32)
    offsets = jnp.where(
        degree_slot < half_degrees, 2 * degree_slot, 2 * (degree_slot - half_degrees) + 1
    )
    inside = offsets[None, None, :] < (degree_count - my_waves)[:, None, None]
    return jnp.where(inside, spectral, jnp.zeros_like(spectral))


def solution(mesh):
    in_specs = (P(("lat", "wave"), None, None), P(), P("wave", "lat", None))
    out_specs = P("wave", None, "lat")
    return jax.shard_map(local, mesh=mesh, in_specs=in_specs, out_specs=out_specs, check_vma=False)
```

profile of v0, /device:TPU:6, one launch (start us, length us, event | category | flops | bytes accessed | tf_op | source)
XLA Modules:
  0.0 185.1 jit_solution(3661106265486786937)
XLA Ops:
  6.5 0.0 reduce-scatter.4.cloned.1.call-start
  6.5 0.7 compare_select_fusion
  7.2 0.7 compare_and_fusion
  7.9 1.3 copy.11
  9.2 4.3 %gather_fusion = bf16[1280,2,12]{2,1,0:T(2,128)(2,1)} fusion(bf16[2,12,1280]{1,0,2:T(2,128)(2,1)S(1)} %copy.11, s32[2048]{0:T(1024)S(1)} %pad_clamp_fusion), kind=kCustom, calls=%fused_computation | custom fusion | bytes 128000 | tf_op jit(solution)/shard_map/jit(_take)/gather | solution.py:23
  13.5 0.0 copy-start
  13.5 7.4 %fusion.8 = bf16[1280,2,12]{2,1,0:T(2,128)(2,1)} fusion(bf16[1280,2,12]{2,1,0:T(2,128)(2,1)} %gather_fusion, pred[1280]{0:T(1024)(128)(4,1)S(1)} %compare_and_fusion), kind=kLoop, calls=%fused_computation.22 | loop fusion | flops 30720 | bytes 124160
  20.9 1.7 reshape.55
  22.6 21.6 %all_to_all.18 = bf16[32,2,480]{2,1,0:T(2,128)(2,1)S(1)} all-to-all(bf16[32,2,480]{2,1,0:T(2,128)(2,1)S(1)} %reshape.55), channel_id=1, replica_groups=mesh['lat'=16,'wave'=32] {'wave'}, dimensions={0} | all-to-all | bytes 122880 | tf_op jit(solution)/shard_map/all_to_all | solution.py:24
  44.1 1.3 reshape.56
  45.5 2.4 %copy.12 = bf16[2,12,32,40]{3,0,2,1:T(2,128)(2,1)S(1)} copy(bf16[2,12,32,40]{1,0,3,2:T(2,128)(2,1)} %bitcast.19) | data formatting | bytes 122880 | tf_op jit(solution)/shard_map/all_to_all | solution.py:24
  47.9 0.7 fusion.7
  48.6 1.9 %collective-permute-start = (bf16[40,12,32]{0,2,1:T(8,128)(2,1)S(1)}, bf16[40,12,32]{0,2,1:T(8,128)(2,1)S(1)}, u32[]{:S(2)}, u32[]{:S(2)}) collective-permute-start(bf16[40,12,32]{0,2,1:T(8,128)(2,1)S(1)} %get-tuple-element.8), channel_id=1, source_target_pairs={{0,32},{32,0},{64,96},{96,64},{128,160},{160,128},{192,224},{224,1... | collective-permute-start | bytes 92168 | tf_op jit(solution)/shard_map/ppermute | solution.py:14
  50.5 1.3 collective-permute-done
  51.7 3.5 %collective-permute-start.1 = (bf16[40,12,32]{0,2,1:T(8,128)(2,1)S(1)}, bf16[40,12,32]{0,2,1:T(8,128)(2,1)S(1)}, u32[]{:S(2)}, u32[]{:S(2)}) collective-permute-start(bf16[40,12,32]{0,2,1:T(8,128)(2,1)S(1)} %collective-permute-done), channel_id=1, source_target_pairs={{0,64},{64,0},{32,96},{96,32},{128,192},{192,128},{160,224},{224,1... | collective-permute-start | bytes 92168 | tf_op jit(solution)/shard_map/ppermute | solution.py:14
  55.2 3.3 %collective-permute-done.1 = bf16[40,12,32]{0,2,1:T(8,128)(2,1)S(1)} collective-permute-done((bf16[40,12,32]{0,2,1:T(8,128)(2,1)S(1)}, bf16[40,12,32]{0,2,1:T(8,128)(2,1)S(1)}, u32[]{:S(2)}, u32[]{:S(2)}) %collective-permute-start.1) | collective-permute-done | bytes 30752 | tf_op jit(solution)/shard_map/ppermute | solution.py:14
  58.5 4.5 %collective-permute-start.2 = (bf16[40,12,32]{0,2,1:T(8,128)(2,1)S(1)}, bf16[40,12,32]{0,2,1:T(8,128)(2,1)}, u32[]{:S(2)}, u32[]{:S(2)}) collective-permute-start(bf16[40,12,32]{0,2,1:T(8,128)(2,1)S(1)} %collective-permute-done.1), channel_id=1, source_target_pairs={{0,128},{128,0},{32,160},{160,32},{64,192},{192,64},{96,224},{224,... | collective-permute-start | bytes 92168 | tf_op jit(solution)/shard_map/ppermute | solution.py:14
  63.0 4.5 %collective-permute-done.2 = bf16[40,12,32]{0,2,1:T(8,128)(2,1)} collective-permute-done((bf16[40,12,32]{0,2,1:T(8,128)(2,1)S(1)}, bf16[40,12,32]{0,2,1:T(8,128)(2,1)}, u32[]{:S(2)}, u32[]{:S(2)}) %collective-permute-start.2) | collective-permute-done | bytes 30752 | tf_op jit(solution)/shard_map/ppermute | solution.py:14
  67.5 7.7 %collective-permute-start.3 = (bf16[40,12,32]{0,2,1:T(8,128)(2,1)}, bf16[40,12,32]{0,2,1:T(8,128)(2,1)}, u32[]{:S(2)}, u32[]{:S(2)}) collective-permute-start(bf16[40,12,32]{0,2,1:T(8,128)(2,1)} %collective-permute-done.2), channel_id=1, source_target_pairs={{0,256},{256,0},{32,288},{288,32},{64,320},{320,64},{96,352},{352,... | collective-permute-start | bytes 92168 | tf_op jit(solution)/shard_map/ppermute | solution.py:14
  75.2 1.6 rev.8
  76.8 2.5 %collective-permute-done.3 = bf16[40,12,32]{0,2,1:T(8,128)(2,1)} collective-permute-done((bf16[40,12,32]{0,2,1:T(8,128)(2,1)}, bf16[40,12,32]{0,2,1:T(8,128)(2,1)}, u32[]{:S(2)}, u32[]{:S(2)}) %collective-permute-start.3) | collective-permute-done | bytes 30752 | tf_op jit(solution)/shard_map/ppermute | solution.py:14
  79.3 1.6 rev.7
  80.8 1.6 fusion.5
  82.4 1.1 copy.14
  83.5 1.7 copy.13
  85.3 0.0 copy-done
  85.3 0.0 copy-start.1
  85.3 0.4 fusion
  85.7 0.5 copy-done.1
  86.2 0.4 fusion.2
  86.6 0.4 pad_maximum_fusion
  87.0 12.4 %copy.16 = f32[40,12,1280]{1,0,2:T(8,128)} copy(f32[40,12,1280]{2,1,0:T(8,128)S(1)} %pad_maximum_fusion) | data formatting | bytes 4915200
  99.4 16.7 %reshape.53 = f32[1280,480]{1,0:T(8,128)} reshape(f32[1280,40,12]{2,1,0:T(8,128)} %bitcast.17) | data formatting | bytes 4915200
  116.1 0.0 reduce-scatter.4.cloned.1.call-update
  116.1 0.8 dynamic-slice_subtract_fusion
  116.9 0.1 broadcast_compare_fusion
  117.0 58.4 %reduce-scatter.4.cloned.1.call-done = f32[80,480]{1,0:T(8,128)} async-done(((f32[1280,480]{1,0:T(8,128)}), f32[80,480]{1,0:T(8,128)}) %reduce-scatter.4.cloned.1.call-update) | async-done | bytes 153616
  175.4 1.4 reshape.54
  176.9 0.6 copy.17
  177.5 0.8 copy.15
  (3 shorter events, 0.1 us)
Async XLA Ops:
  6.5 168.9 %reduce-scatter.4.cloned.1.call-start = ((), (), s32[]{:S(2)}) async-start(), calls=%async_computation.2 | async-start | bytes 2785280
  13.5 71.8 %copy-start = (bf16[40,32,1280]{2,1,0:T(8,128)(2,1)S(1)}, bf16[40,32,1280]{2,1,0:T(8,128)(2,1)}, u32[]{:S(2)}) copy-start(bf16[40,32,1280]{2,1,0:T(8,128)(2,1)} %param.5) | copy-start | bytes 9830404
  48.6 3.2 %collective-permute-start = (bf16[40,12,32]{0,2,1:T(8,128)(2,1)S(1)}, bf16[40,12,32]{0,2,1:T(8,128)(2,1)S(1)}, u32[]{:S(2)}, u32[]{:S(2)}) collective-permute-start(bf16[40,12,32]{0,2,1:T(8,128)(2,1)S(1)} %get-tuple-element.8), channel_id=1, source_target_pairs={{0,32},{32,0},{64,96},{96,64},{128,160},{160,128},{192,224},{224,1... | collective-permute-start | bytes 92168 | tf_op jit(solution)/shard_map/ppermute | solution.py:14
  51.7 6.7 %collective-permute-start.1 = (bf16[40,12,32]{0,2,1:T(8,128)(2,1)S(1)}, bf16[40,12,32]{0,2,1:T(8,128)(2,1)S(1)}, u32[]{:S(2)}, u32[]{:S(2)}) collective-permute-start(bf16[40,12,32]{0,2,1:T(8,128)(2,1)S(1)} %collective-permute-done), channel_id=1, source_target_pairs={{0,64},{64,0},{32,96},{96,32},{128,192},{192,128},{160,224},{224,1... | collective-permute-start | bytes 92168 | tf_op jit(solution)/shard_map/ppermute | solution.py:14
  58.5 9.0 %collective-permute-start.2 = (bf16[40,12,32]{0,2,1:T(8,128)(2,1)S(1)}, bf16[40,12,32]{0,2,1:T(8,128)(2,1)}, u32[]{:S(2)}, u32[]{:S(2)}) collective-permute-start(bf16[40,12,32]{0,2,1:T(8,128)(2,1)S(1)} %collective-permute-done.1), channel_id=1, source_target_pairs={{0,128},{128,0},{32,160},{160,32},{64,192},{192,64},{96,224},{224,... | collective-permute-start | bytes 92168 | tf_op jit(solution)/shard_map/ppermute | solution.py:14
  67.5 11.8 %collective-permute-start.3 = (bf16[40,12,32]{0,2,1:T(8,128)(2,1)}, bf16[40,12,32]{0,2,1:T(8,128)(2,1)}, u32[]{:S(2)}, u32[]{:S(2)}) collective-permute-start(bf16[40,12,32]{0,2,1:T(8,128)(2,1)} %collective-permute-done.2), channel_id=1, source_target_pairs={{0,256},{256,0},{32,288},{288,32},{64,320},{320,64},{96,352},{352,... | collective-permute-start | bytes 92168 | tf_op jit(solution)/shard_map/ppermute | solution.py:14
  85.3 0.9 copy-start.1
Sparse Core Ops, SparseCore 0:
  116.3 59.1 reduce-scatter.3
where the time goes:
time: 186 us; the launch traced here: 185 us
  waiting for transfers between devices  69.9 us (38%)
  local copies, waits for them, and re-layouts  49.9 us (27%)
  blocking collectives  21.6 us (12%)
  starting transfers between devices  17.6 us (9%)
  between operations  13.5 us (7%)
  other arithmetic  11.7 us (6%)
    unnamed x2, waiting for transfers between devices  58.4 us
    unnamed x11, local copies, waits for them, and re-layouts  35.9 us
    all_to_all x1, blocking collectives, local(): lax.all_to_all(ordered, 'wave', split_axis=2, concat_axis=0, tiled=True)  21.6 us
    ppermute x4, starting transfers between devices, partner(): return lax.ppermute(block, axis, route)  17.6 us
    ppermute x4, waiting for transfers between devices, partner(): return lax.ppermute(block, axis, route)  11.5 us
    unnamed x1, other arithmetic  7.39 us
    gather x1, local copies, waits for them, and re-layouts, local(): ordered = jnp.take(fourier, wave_table, axis=2)  4.25 us
  transfers between devices with their start and end apart: 5, of which 5 were waited for; matrix products, arithmetic and copies ran while one was open for 1% of the time, Pallas kernels for 0%

commit v1 on v0

v1 whole, which is shorter than its diff:
```python
import functools

import jax
import jax.numpy as jnp
from jax import lax
from jax.experimental import pallas as pl
from jax.experimental.pallas import tpu as pltpu
from jax.sharding import PartitionSpec as P

MESH = pl.DeviceIdType.MESH
F32, BF16, I32 = jnp.float32, jnp.bfloat16, jnp.int32

LATS, WAVES, CHIPS = 16, 32, 8
SLOTS, COLS, PAIRS, DEG = 40, 12, 32, 1280
OWN = 80
ROWS = 304
GROUPS = 5
PIECES = ((0, 304),)


def lanes(shape):
    return lax.broadcasted_iota(I32, shape, len(shape) - 1)


def kernel(fo_hbm, wt_hbm, leg_hbm, out_ref, fo, wt, leg, vg, snd, ns, eo, lhs, lim,
           part, sib, rsnd, rrcv, in_sem, a_send, a_recv, s_send, s_recv, r_send, r_recv):
    lat = lax.axis_index("lat")
    wave = lax.axis_index("wave")
    chip, core = lat // 2, lat % 2
    step = 1 - 2 * core
    mirror = LATS - 1 - lat
    half = wave // 16
    target_lat = jnp.where(half == 1, mirror, lat)

    def chip_at(distance):
        return (chip + distance * step + 2 * CHIPS) % CHIPS

    up = chip_at(1)

    load_fo = pltpu.make_async_copy(fo_hbm, fo, in_sem.at[0])
    load_wt = pltpu.make_async_copy(wt_hbm, wt, in_sem.at[1])
    load_leg = pltpu.make_async_copy(leg_hbm, leg, in_sem.at[2])
    load_fo.start()
    load_wt.start()
    load_leg.start()

    barrier = pltpu.get_barrier_semaphore()

    def greet(d, carry):
        other = (wave + d) % WAVES
        at = jnp.where(other < 16, lat, mirror)
        pl.semaphore_signal(barrier, inc=1, device_id=(at, other), device_id_type=MESH)
        return carry

    lax.fori_loop(1, WAVES, greet, 0)

    @pl.when(half == 1)
    def _():
        pl.semaphore_signal(barrier, inc=1, device_id=(mirror, wave), device_id_type=MESH)

    pl.semaphore_signal(barrier, inc=1, device_id=(lat + step, wave), device_id_type=MESH)
    below, above = (chip + CHIPS - 1) % CHIPS, (chip + 1) % CHIPS
    pl.semaphore_signal(barrier, inc=1, device_id=(2 * below, wave), device_id_type=MESH)
    pl.semaphore_signal(barrier, inc=1, device_id=(2 * above + 1, wave), device_id_type=MESH)

    load_fo.wait()
    load_wt.wait()
    south = lat >= LATS // 2
    first, second = fo[0].astype(F32), fo[1].astype(F32)
    row_a = jnp.where(south, second, first)
    row_b = jnp.where(south, first, second)
    for g in range(3):
        vg[g] = jnp.concatenate([row_a[4 * g:4 * g + 4], row_b[4 * g:4 * g + 4]], axis=0)
    lane8 = lanes((8, 128))

    def table_lanes(start):
        row, off = start // 128, start % 128
        back = (128 - off) % 128
        near = jnp.broadcast_to(wt[pl.ds(row, 1), :], (8, 128))
        far = jnp.broadcast_to(wt[pl.ds(jnp.minimum(row + 1, 9), 1), :], (8, 128))
        return jnp.where(lane8 < 128 - off, pltpu.roll(near, back, 1), pltpu.roll(far, back, 1))

    def pick(t, carry):
        index = table_lanes(120 * t)
        low, high = index & 127, index >> 7
        found = []
        for g in range(3):
            acc = jnp.zeros((8, 128), F32)
            for u in range(10):
                got = jnp.take_along_axis(vg[g, :, 128 * u:128 * u + 128], low, axis=1,
                                          mode="promise_in_bounds")
                acc = jnp.where(high == u, got, acc)
            found.append(acc)
        for d in range(3):
            turned = [found[g] if g == d else pltpu.roll(found[g], (40 * (g - d)) % 128, 1)
                      for g in range(3)]
            message = jnp.where(lane8 < 40, turned[0], jnp.where(lane8 < 80, turned[1], turned[2]))
            snd[3 * t + d] = message.astype(BF16)
        return carry

    lax.fori_loop(0, 11, pick, 0)

    mine = jnp.broadcast_to(table_lanes(SLOTS * wave)[0:1].astype(F32), (128, 128))
    lim[...] = DEG - mine.T[:SLOTS]

    pl.semaphore_wait(barrier, 34 + half)

    place = jnp.where(south, 16 + 15 - wave % 16, wave % 16)

    def exchange(d):
        to = (wave + d) % WAVES
        return pltpu.make_async_remote_copy(
            src_ref=snd.at[to], dst_ref=ns.at[place], send_sem=a_send.at[d],
            recv_sem=a_recv.at[place], device_id=(target_lat, to), device_id_type=MESH)

    def start_exchange(d, carry):
        exchange(d).start()
        return carry

    lax.fori_loop(1, WAVES, start_exchange, 0)
    stay = pltpu.make_async_copy(snd.at[wave], ns.at[place], a_recv.at[place])

    @pl.when(half == 1)
    def _():
        exchange(0).start()

    @pl.when(half == 0)
    def _():
        stay.start()

    load_leg.wait()

    def arrive(s, carry):
        pltpu.make_async_copy(snd.at[0], ns.at[s], a_recv.at[s]).wait()
        return carry

    lax.fori_loop(0, WAVES, arrive, 0)

    north = ns[0:16].astype(F32)
    southern = ns[16:32].astype(F32)
    eo[0] = (north + southern).astype(BF16).astype(F32).reshape(128, 128)
    eo[1] = (north - southern).astype(BF16).astype(F32).reshape(128, 128)
    sub = lax.broadcasted_iota(I32, (8, 128), 0)
    keep = [sub == 4 * kt + lane8 // 32 for kt in range(2)]
    for part_of in range(2):
        for pair in range(2):
            turned = []
            for c4 in (2 * pair, 2 * pair + 1):
                x = eo[part_of, pl.ds(c4, 32, stride=4), :]
                turned.append(jnp.concatenate([x] * 4, axis=0).T)
            for g in range(3):
                c = 4 * g + 2 * pair
                for q in range(GROUPS):
                    at = 40 * g + 8 * q
                    for kt in range(2):
                        both = jnp.concatenate(
                            [jnp.where(keep[kt], t[at:at + 8], 0.0) for t in turned], axis=0)
                        lhs[part_of, q, 8 * c:8 * c + 16, 128 * kt:128 * kt + 128] = both.astype(BF16)

    lane96 = lanes((96, 128))

    def product(job, owner):
        off = 32 * (owner % 4)
        column = pl.multiple_of(128 * ((5 * owner) // 4), 128)
        placed = [[], []]
        for q in range(GROUPS):
            right = leg[8 * q:8 * q + 8, :, pl.ds(column, 256)].reshape(256, 256)
            got = jnp.dot(lhs[owner // 4, q], right, preferred_element_type=F32)
            for e in range(2):
                start = off + OWN * e
                window = jnp.where(lane96 >= start, got[:, :128], got[:, 128:])
                placed[e].append(pltpu.roll(window, (OWN * q + 256 - start) % 128, 1))
        for e in range(2):
            z = placed[e]
            part[job, e, 0:96] = jnp.where(lane96 < 80, z[0], z[1])
            part[job, e, 96:192] = jnp.where(lane96 < 32, z[1], jnp.where(lane96 < 112, z[2], z[3]))
            part[job, e, 192:288] = jnp.where(lane96 < 64, z[3], z[4])
            for v, count in ((0, 8), (1, 4)):
                rest = z[4][64 * v:64 * v + 8]
                for n in range(1, count):
                    c = 8 * v + n
                    rest = jnp.where(lane8 // 16 == n, pltpu.roll(z[4][8 * c:8 * c + 8], 16 * n, 1), rest)
                part[job, e, 288 + 8 * v:296 + 8 * v] = rest

    def to_sibling(job, e, slot):
        return pltpu.make_async_remote_copy(
            src_ref=part.at[job, e], dst_ref=sib.at[slot], send_sem=s_send.at[slot],
            recv_sem=s_recv.at[slot], device_id=(lat + step, wave), device_id_type=MESH)

    def ring(slot, piece, at_lat, to_slot):
        low, high = PIECES[piece]
        return pltpu.make_async_remote_copy(
            src_ref=rsnd.at[slot, low:high], dst_ref=rrcv.at[to_slot, low:high],
            send_sem=r_send.at[slot, piece], recv_sem=r_recv.at[to_slot, piece],
            device_id=(at_lat, wave), device_id_type=MESH)

    same = 2 * up + core

    def pass_on(slot, job, e, from_sib, arrived, at_lat, to_slot):
        for piece, (low, high) in enumerate(PIECES):
            total = part[job, e, low:high] + sib[from_sib, low:high]
            if arrived is not None:
                ring(0, piece, same, arrived).wait_recv()
                total = total + rrcv[arrived, low:high].astype(F32)
            rsnd[slot, low:high] = total.astype(BF16)
            ring(slot, piece, at_lat, to_slot).start()

    other = 1 - core

    def work(job, carry):
        toward = job % 2 == 0
        far = jnp.where(job == 0, 4, jnp.where(job == 7, 0, 3 - (job - 1) // 2))
        owner = chip_at(jnp.where(toward, far, -far))
        product(job, owner)

        @pl.when(job == 0)
        def _():
            to_sibling(0, other, 0).start()

        for k in (1, 3, 5):
            @pl.when(job == k)
            def _():
                to_sibling(k, 0, k).start()
                to_sibling(k, 1, k + 1).start()

        @pl.when(job == 7)
        def _():
            to_sibling(7, other, 7).start()

        @pl.when(job == 1)
        def _():
            to_sibling(0, other, 0).wait_recv()
            pass_on(0, 0, core, 0, None, same, 0)

        @pl.when(job == 2)
        def _():
            to_sibling(1, 0, 1).wait_recv()
            to_sibling(1, 1, 2).wait_recv()
            pass_on(1 + other, 2, other, 1 + other, None, same, 1 + other)

        @pl.when(job == 3)
        def _():
            pass_on(1 + core, 2, core, 1 + core, 0, same, 1 + core)

        @pl.when(job == 4)
        def _():
            to_sibling(3, 0, 3).wait_recv()
            to_sibling(3, 1, 4).wait_recv()
            pass_on(3 + other, 4, other, 3 + other, 1 + other, same, 3 + other)

        @pl.when(job == 5)
        def _():
            pass_on(3 + core, 4, core, 3 + core, 1 + core, same, 3 + core)

        @pl.when(job == 6)
        def _():
            to_sibling(5, 0, 5).wait_recv()
            to_sibling(5, 1, 6).wait_recv()
            pass_on(5 + other, 6, other, 5 + other, 3 + other, 2 * up + other, 5 + core)

        @pl.when(job == 7)
        def _():
            pass_on(5 + core, 6, core, 5 + core, 3 + core, 2 * up + core, 5 + core)

        return carry

    lax.fori_loop(0, 8, work, 0)

    to_sibling(7, other, 7).wait_recv()
    for slot in (5, 6):
        for piece in range(len(PIECES)):
            ring(0, piece, same, slot).wait_recv()

    def total(low, high):
        return (part[7, core, low:high] + sib[7, low:high]
                + rrcv[5, low:high].astype(F32) + rrcv[6, low:high].astype(F32))

    t0, t1, t2, rest = total(0, 96), total(96, 192), total(192, 288), total(288, 304)
    spread = jnp.concatenate(
        [rest[8 * (c // 8):8 * (c // 8) + 8] if c % 8 == 0
         else pltpu.roll(rest[8 * (c // 8):8 * (c // 8) + 8], 128 - 16 * (c % 8), 1)
         for c in range(COLS)], axis=0)
    z = [t0,
         pltpu.roll(jnp.where(lane96 >= 80, t0, t1), 48, 1),
         pltpu.roll(t1, 96, 1),
         pltpu.roll(jnp.where(lane96 >= 112, t1, t2), 16, 1),
         pltpu.roll(jnp.where(lane96 >= 64, t2, spread), 64, 1)]
    degree = OWN * lat + lane8
    offset = jnp.where(degree < DEG // 2, 2 * degree, 2 * degree - (DEG - 1)).astype(F32)
    for q in range(GROUPS):
        inside = offset < lim[8 * q:8 * q + 8]
        for c in range(COLS):
            value = jnp.where(inside, z[q][8 * c:8 * c + 8], 0.0)
            out_ref[c, 8 * q:8 * q + 8, :] = value[:, :OWN]

    def sent(d, carry):
        exchange(d).wait_send()
        return carry

    lax.fori_loop(1, WAVES, sent, 0)

    @pl.when(half == 1)
    def _():
        exchange(0).wait_send()

    for slot in range(8):
        to_sibling(0, 0, slot).wait_send()
    for slot in range(7):
        for piece in range(len(PIECES)):
            ring(slot, piece, same, 0).wait_send()


def local(fourier, wave_table, legendre):
    table = wave_table.reshape(10, 128)
    hbm = pl.BlockSpec(memory_space=pltpu.MemorySpace.HBM)
    out = pl.pallas_call(
        kernel,
        out_shape=jax.ShapeDtypeStruct((COLS, SLOTS, OWN), F32),
        in_specs=[hbm, hbm, hbm],
        out_specs=pl.BlockSpec(memory_space=pltpu.VMEM),
        scratch_shapes=[
            pltpu.VMEM((2, COLS, DEG), BF16),
            pltpu.VMEM((10, 128), I32),
            pltpu.VMEM((SLOTS, PAIRS, DEG), BF16),
            pltpu.VMEM((3, 8, DEG), F32),
            pltpu.VMEM((33, 8, 128), BF16),
            pltpu.VMEM((32, 8, 128), BF16),
            pltpu.VMEM((2, 128, 128), F32),
            pltpu.VMEM((2, GROUPS, 96, 256), BF16),
            pltpu.VMEM((SLOTS, 128), F32),
            pltpu.VMEM((8, 2, ROWS, 128), F32),
            pltpu.VMEM((8, ROWS, 128), F32),
            pltpu.VMEM((7, ROWS, 128), BF16),
            pltpu.VMEM((7, ROWS, 128), BF16),
            pltpu.SemaphoreType.DMA((3,)),
            pltpu.SemaphoreType.DMA((WAVES,)),
            pltpu.SemaphoreType.DMA((WAVES,)),
            pltpu.SemaphoreType.DMA((8,)),
            pltpu.SemaphoreType.DMA((8,)),
            pltpu.SemaphoreType.DMA((7, len(PIECES))),
            pltpu.SemaphoreType.DMA((7, len(PIECES))),
        ],
        compiler_params=pltpu.CompilerParams(
            collective_id=0, has_side_effects=True, vmem_limit_bytes=48 << 20),
        name="legendre",
    )(fourier, table, legendre)
    return jnp.transpose(out, (1, 0, 2))


def solution(mesh):
    in_specs = (P(("lat", "wave"), None, None), P(), P("wave", "lat", None))
    out_specs = P("wave", None, "lat")
    return jax.shard_map(local, mesh=mesh, in_specs=in_specs, out_specs=out_specs, check_vma=False)
```

time: 186 us -> 46 us (0.25)
  the two profiles are of different devices: /device:TPU:6 before, /device:TPU:8 now
where the time goes in v1:
time: 46 us; the launch traced here: 45.7 us
  Pallas kernels  41.6 us (90%)
  local copies, waits for them, and re-layouts  4.15 us (9%)
    pallas_call x1, Pallas kernels, local(): pl.pallas_call(kernel, out_shape=jax.ShapeDtypeStruct((COLS, SLOTS, OWN),...  41.6 us
    unnamed x6, local copies, waits for them, and re-layouts  4.15 us

profile of v1, /device:TPU:8, one launch (start us, length us, event | category | flops | bytes accessed | tf_op | source)
XLA Modules:
  0.0 45.7 jit_solution(16889874237695905020)
XLA Ops:
  0.0 0.8 %copy.4.fo_hbm = bf16[2,12,1280]{2,1,0:T(8,128)(2,1)S(1)} copy(bf16[2,12,1280]{2,0,1:T(2,128)(2,1)} %param.3) | data formatting | bytes 122880 | tf_op args[0]
  0.8 0.0 copy-start
  0.9 1.9 %copy-done = bf16[40,32,1280]{2,1,0:T(8,128)(2,1)S(1)} copy-done((bf16[40,32,1280]{2,1,0:T(8,128)(2,1)S(1)}, bf16[40,32,1280]{2,1,0:T(8,128)(2,1)}, u32[]{:S(2)}) %copy-start) | copy-done | bytes 3276824
  2.8 0.0 copy-start.1
  2.8 0.7 %copy-done.1 = s32[1280]{0:T(1024)S(1)} copy-done((s32[1280]{0:T(1024)S(1)}, s32[1280]{0:T(1024)}, u32[]{:S(2)}) %copy-start.1) | copy-done | bytes 5144
  3.5 41.6 %legendre.1 = f32[12,40,80]{2,1,0:T(8,128)S(1)} custom-call(bf16[2,12,1280]{2,1,0:T(8,128)(2,1)S(1)} %copy.4.fo_hbm, s32[10,128]{1,0:T(8,128)S(1)} %bitcast.3, bf16[40,32,1280]{2,1,0:T(8,128)(2,1)S(1)} %copy-done), custom_call_target="tpu_custom_call" | custom-call | tf_op jit(solution)/shard_map/legendre/pallas_call | solution.py:316
  45.0 0.7 %copy.6 = f32[40,12,80]{2,0,1:T(8,128)} copy(f32[40,12,80]{2,0,1:T(8,128)S(1)} %bitcast.2) | data formatting | bytes 307200
Async XLA Ops:
  0.8 1.9 %copy-start = (bf16[40,32,1280]{2,1,0:T(8,128)(2,1)S(1)}, bf16[40,32,1280]{2,1,0:T(8,128)(2,1)}, u32[]{:S(2)}) copy-start(bf16[40,32,1280]{2,1,0:T(8,128)(2,1)} %leg_hbm.1) | copy-start | bytes 9830404
  2.8 0.7 %copy-start.1 = (s32[1280]{0:T(1024)S(1)}, s32[1280]{0:T(1024)}, u32[]{:S(2)}) copy-start(s32[1280]{0:T(1024)} %param.4) | copy-start | bytes 15364

commit v2 on v1

--- a/solution.py
+++ b/solution.py
@@ -1,5 +1,3 @@
-import functools
-
 import jax
 import jax.numpy as jnp
 from jax import lax
@@ -15,7 +13,7 @@
 OWN = 80
 ROWS = 304
 GROUPS = 5
-PIECES = ((0, 304),)
+PIECES = ((0, 160), (160, 304))
 
 
 def lanes(shape):
@@ -59,14 +57,16 @@
         pl.semaphore_signal(barrier, inc=1, device_id=(mirror, wave), device_id_type=MESH)
 
     pl.semaphore_signal(barrier, inc=1, device_id=(lat + step, wave), device_id_type=MESH)
-    below, above = (chip + CHIPS - 1) % CHIPS, (chip + 1) % CHIPS
-    pl.semaphore_signal(barrier, inc=1, device_id=(2 * below, wave), device_id_type=MESH)
-    pl.semaphore_signal(barrier, inc=1, device_id=(2 * above + 1, wave), device_id_type=MESH)
+    for away in (1, 2):
+        for way in range(2):
+            back = (chip + CHIPS - away * (1 - 2 * way)) % CHIPS
+            pl.semaphore_signal(barrier, inc=1, device_id=(2 * back + way, wave), device_id_type=MESH)
 
     load_fo.wait()
     load_wt.wait()
     south = lat >= LATS // 2
-    first, second = fo[0].astype(F32), fo[1].astype(F32)
+    rows = fo[...].astype(F32)
+    first, second = rows[:, 0, :], rows[:, 1, :]
     row_a = jnp.where(south, second, first)
     row_b = jnp.where(south, first, second)
     for g in range(3):
@@ -103,12 +103,15 @@
     mine = jnp.broadcast_to(table_lanes(SLOTS * wave)[0:1].astype(F32), (128, 128))
     lim[...] = DEG - mine.T[:SLOTS]
 
-    pl.semaphore_wait(barrier, 34 + half)
+    pl.semaphore_wait(barrier, 36 + half)
 
     place = jnp.where(south, 16 + 15 - wave % 16, wave % 16)
 
     def exchange(d):
-        to = (wave + d) % WAVES
+        kz, kx = d // 4, d % 4
+        dz = 4 + ((kz + 1) // 2) * (2 * (kz % 2) - 1) + 8
+        dx = 2 + ((kx + 1) // 2) * (2 * (kx % 2) - 1) + 4
+        to = 4 * ((wave // 4 + dz) % 8) + (wave + dx) % 4
         return pltpu.make_async_remote_copy(
             src_ref=snd.at[to], dst_ref=ns.at[place], send_sem=a_send.at[d],
             recv_sem=a_recv.at[place], device_id=(target_lat, to), device_id_type=MESH)
@@ -117,12 +120,12 @@
         exchange(d).start()
         return carry
 
-    lax.fori_loop(1, WAVES, start_exchange, 0)
+    lax.fori_loop(0, WAVES - 1, start_exchange, 0)
     stay = pltpu.make_async_copy(snd.at[wave], ns.at[place], a_recv.at[place])
 
     @pl.when(half == 1)
     def _():
-        exchange(0).start()
+        exchange(WAVES - 1).start()
 
     @pl.when(half == 0)
     def _():
@@ -194,17 +197,16 @@
             send_sem=r_send.at[slot, piece], recv_sem=r_recv.at[to_slot, piece],
             device_id=(at_lat, wave), device_id_type=MESH)
 
-    same = 2 * up + core
-
     def pass_on(slot, job, e, from_sib, arrived, at_lat, to_slot):
         for piece, (low, high) in enumerate(PIECES):
             total = part[job, e, low:high] + sib[from_sib, low:high]
-            if arrived is not None:
-                ring(0, piece, same, arrived).wait_recv()
-                total = total + rrcv[arrived, low:high].astype(F32)
+            for had in arrived:
+                ring(0, piece, at_lat, had).wait_recv()
+                total = total + rrcv[had, low:high].astype(F32)
             rsnd[slot, low:high] = total.astype(BF16)
             ring(slot, piece, at_lat, to_slot).start()
 
+    one, two = 2 * up, 2 * chip_at(2)
     other = 1 - core
 
     def work(job, carry):
@@ -227,52 +229,41 @@
         def _():
             to_sibling(7, other, 7).start()
 
-        @pl.when(job == 1)
+        @pl.when(job == 2)
         def _():
             to_sibling(0, other, 0).wait_recv()
-            pass_on(0, 0, core, 0, None, same, 0)
-
-        @pl.when(job == 2)
-        def _():
+            pass_on(0, 0, core, 0, (), two + core, 0)
             to_sibling(1, 0, 1).wait_recv()
+            pass_on(1, 2, 0, 1, (), one + core, 1)
             to_sibling(1, 1, 2).wait_recv()
-            pass_on(1 + other, 2, other, 1 + other, None, same, 1 + other)
-
-        @pl.when(job == 3)
-        def _():
-            pass_on(1 + core, 2, core, 1 + core, 0, same, 1 + core)
-
-        @pl.when(job == 4)
+            pass_on(2, 2, 1, 2, (), one + core, 2)
+
+        @pl.when(job == 6)
+        def _():
+            to_sibling(5, 0, 5).wait_recv()
+            pass_on(3, 6, 0, 5, (), one, 3 + core)
+            to_sibling(5, 1, 6).wait_recv()
+            pass_on(4, 6, 1, 6, (), one + 1, 3 + core)
+
+        @pl.when(job == 7)
         def _():
             to_sibling(3, 0, 3).wait_recv()
             to_sibling(3, 1, 4).wait_recv()
-            pass_on(3 + other, 4, other, 3 + other, 1 + other, same, 3 + other)
-
-        @pl.when(job == 5)
-        def _():
-            pass_on(3 + core, 4, core, 3 + core, 1 + core, same, 3 + core)
-
-        @pl.when(job == 6)
-        def _():
-            to_sibling(5, 0, 5).wait_recv()
-            to_sibling(5, 1, 6).wait_recv()
-            pass_on(5 + other, 6, other, 5 + other, 3 + other, 2 * up + other, 5 + core)
-
-        @pl.when(job == 7)
-        def _():
-            pass_on(5 + core, 6, core, 5 + core, 3 + core, 2 * up + core, 5 + core)
+            pass_on(5 + other, 4, other, 3 + other, (1 + other,), two + other, 5 + core)
+            pass_on(5 + core, 4, core, 3 + core, (1 + core, 0), two + core, 5 + core)
 
         return carry
 
     lax.fori_loop(0, 8, work, 0)
 
     to_sibling(7, other, 7).wait_recv()
-    for slot in (5, 6):
+    for slot in range(3, 7):
         for piece in range(len(PIECES)):
-            ring(0, piece, same, slot).wait_recv()
+            ring(0, piece, one, slot).wait_recv()
 
     def total(low, high):
         return (part[7, core, low:high] + sib[7, low:high]
+                + rrcv[3, low:high].astype(F32) + rrcv[4, low:high].astype(F32)
                 + rrcv[5, low:high].astype(F32) + rrcv[6, low:high].astype(F32))
 
     t0, t1, t2, rest = total(0, 96), total(96, 192), total(192, 288), total(288, 304)
@@ -297,17 +288,17 @@
         exchange(d).wait_send()
         return carry
 
-    lax.fori_loop(1, WAVES, sent, 0)
+    lax.fori_loop(0, WAVES - 1, sent, 0)
 
     @pl.when(half == 1)
     def _():
-        exchange(0).wait_send()
+        exchange(WAVES - 1).wait_send()
 
     for slot in range(8):
         to_sibling(0, 0, slot).wait_send()
     for slot in range(7):
         for piece in range(len(PIECES)):
-            ring(slot, piece, same, 0).wait_send()
+            ring(slot, piece, one, 0).wait_send()
 
 
 def local(fourier, wave_table, legendre):
@@ -319,7 +310,7 @@
         in_specs=[hbm, hbm, hbm],
         out_specs=pl.BlockSpec(memory_space=pltpu.VMEM),
         scratch_shapes=[
-            pltpu.VMEM((2, COLS, DEG), BF16),
+            pltpu.VMEM((COLS, 2, DEG), BF16),
             pltpu.VMEM((10, 128), I32),
             pltpu.VMEM((SLOTS, PAIRS, DEG), BF16),
             pltpu.VMEM((3, 8, DEG), F32),
@@ -341,9 +332,9 @@
             pltpu.SemaphoreType.DMA((7, len(PIECES))),
         ],
         compiler_params=pltpu.CompilerParams(
-            collective_id=0, has_side_effects=True, vmem_limit_bytes=48 << 20),
+            collective_id=0, has_side_effects=True, vmem_limit_bytes=52 << 20),
         name="legendre",
-    )(fourier, table, legendre)
+    )(jnp.transpose(fourier, (1, 0, 2)), table, legendre)
     return jnp.transpose(out, (1, 0, 2))
 
 

time: 46 us -> 41.3 us (0.90)
  Pallas kernels: 41.6 us -> 38.8 us
  local copies, waits for them, and re-layouts: 4.15 us -> 2.22 us
    pallas_call x1, Pallas kernels: 41.6 us -> 38.8 us  [local(): pl.pallas_call(kernel, out_shape=jax.ShapeDtypeStruct((COLS, SLOTS, OWN),...]
    unnamed x6 -> x5, local copies, waits for them, and re-layouts: 4.15 us -> 2.22 us
where the time goes in v2:
time: 41.3 us; the launch traced here: 41.1 us
  Pallas kernels  38.8 us (94%)
  local copies, waits for them, and re-layouts  2.22 us (5%)
    pallas_call x1, Pallas kernels, local(): pl.pallas_call(kernel, out_shape=jax.ShapeDtypeStruct((COLS, SLOTS, OWN),...  38.8 us
    unnamed x5, local copies, waits for them, and re-layouts  2.22 us

profile of v2, /device:TPU:8, one launch (start us, length us, event | category | flops | bytes accessed | tf_op | source)
XLA Modules:
  0.0 41.1 jit_solution(1213551954946631531)
XLA Ops:
  0.0 0.0 copy-start
  0.0 0.8 %copy-done = bf16[2,12,1280]{2,0,1:T(2,128)(2,1)S(1)} copy-done((bf16[2,12,1280]{2,0,1:T(2,128)(2,1)S(1)}, bf16[2,12,1280]{2,0,1:T(2,128)(2,1)}, u32[]{:S(2)}) %copy-start) | copy-done | bytes 61464
  0.8 0.0 copy-start.1
  0.8 0.7 %copy-done.1 = s32[1280]{0:T(1024)S(1)} copy-done((s32[1280]{0:T(1024)S(1)}, s32[1280]{0:T(1024)}, u32[]{:S(2)}) %copy-start.1) | copy-done | bytes 5144
  1.5 38.8 %legendre.1 = f32[12,40,80]{2,1,0:T(8,128)S(1)} custom-call(bf16[12,2,1280]{2,1,0:T(2,128)(2,1)S(1)} %bitcast.4, s32[10,128]{1,0:T(8,128)S(1)} %bitcast.5, bf16[40,32,1280]{2,1,0:T(8,128)(2,1)} %leg_hbm.1), custom_call_target="tpu_custom_call" | custom-call | tf_op jit(solution)/shard_map/legendre/pallas_call | solution.py:307
  40.4 0.7 %copy.5 = f32[40,12,80]{2,0,1:T(8,128)} copy(f32[40,12,80]{2,0,1:T(8,128)S(1)} %bitcast.3) | data formatting | bytes 307200
Async XLA Ops:
  0.0 0.8 %copy-start = (bf16[2,12,1280]{2,0,1:T(2,128)(2,1)S(1)}, bf16[2,12,1280]{2,0,1:T(2,128)(2,1)}, u32[]{:S(2)}) copy-start(bf16[2,12,1280]{2,0,1:T(2,128)(2,1)} %param.3) | copy-start | bytes 184324
  0.8 0.7 %copy-start.1 = (s32[1280]{0:T(1024)S(1)}, s32[1280]{0:T(1024)}, u32[]{:S(2)}) copy-start(s32[1280]{0:T(1024)} %param.4) | copy-start | bytes 15364

commit v3 on v2

--- a/solution.py
+++ b/solution.py
@@ -98,7 +98,7 @@
             snd[3 * t + d] = message.astype(BF16)
         return carry
 
-    lax.fori_loop(0, 11, pick, 0)
+    lax.fori_loop(0, 11, pick, 0, unroll=True)
 
     mine = jnp.broadcast_to(table_lanes(SLOTS * wave)[0:1].astype(F32), (128, 128))
     lim[...] = DEG - mine.T[:SLOTS]
@@ -334,7 +334,7 @@
         compiler_params=pltpu.CompilerParams(
             collective_id=0, has_side_effects=True, vmem_limit_bytes=52 << 20),
         name="legendre",
-    )(jnp.transpose(fourier, (1, 0, 2)), table, legendre)
+    )(*[pltpu.with_memory_space_constraint(a, pltpu.MemorySpace.HBM) for a in (jnp.transpose(fourier, (1, 0, 2)), table, legendre)])
     return jnp.transpose(out, (1, 0, 2))
 
 

time: 41.3 us -> 39.6 us (0.959)
  local copies, waits for them, and re-layouts: 2.22 us -> 0.7 us
    unnamed x5 -> x1, local copies, waits for them, and re-layouts: 2.22 us -> 0.7 us
where the time goes in v3:
time: 39.6 us; the launch traced here: 39.5 us
  Pallas kernels  38.8 us (98%)
  local copies, waits for them, and re-layouts  0.7 us (2%)
    pallas_call x1, Pallas kernels, local(): pl.pallas_call(kernel, out_shape=jax.ShapeDtypeStruct((COLS, SLOTS, OWN),...  38.8 us

profile of v3, /device:TPU:8, one launch (start us, length us, event | category | flops | bytes accessed | tf_op | source)
XLA Modules:
  0.0 39.5 jit_solution(10298565081327201958)
XLA Ops:
  0.0 38.8 %legendre.1 = f32[12,40,80]{2,1,0:T(8,128)S(1)} custom-call(bf16[12,2,1280]{2,1,0:T(2,128)(2,1)} %bitcast.4, s32[10,128]{1,0:T(8,128)} %bitcast.5, bf16[40,32,1280]{2,1,0:T(8,128)(2,1)} %leg_hbm.1), custom_call_target="tpu_custom_call" | custom-call | tf_op jit(solution)/shard_map/legendre/pallas_call | solution.py:307
  38.8 0.7 %copy.5 = f32[40,12,80]{2,0,1:T(8,128)} copy(f32[40,12,80]{2,0,1:T(8,128)S(1)} %bitcast.3) | data formatting | bytes 307200

commit v4 on v3

--- a/solution.py
+++ b/solution.py
@@ -20,8 +20,8 @@
     return lax.broadcasted_iota(I32, shape, len(shape) - 1)
 
 
-def kernel(fo_hbm, wt_hbm, leg_hbm, out_ref, fo, wt, leg, vg, snd, ns, eo, lhs, lim,
-           part, sib, rsnd, rrcv, in_sem, a_send, a_recv, s_send, s_recv, r_send, r_recv):
+def kernel(fo_hbm, wt_hbm, leg_hbm, out_ref, fo, wt, leg, vg, snd, ns, eo, both, lhs, lim,
+           part, rsnd, rrcv, in_sem, a_send, a_recv, x_send, x_recv, r_send, r_recv):
     lat = lax.axis_index("lat")
     wave = lax.axis_index("wave")
     chip, core = lat // 2, lat % 2
@@ -37,7 +37,7 @@
 
     load_fo = pltpu.make_async_copy(fo_hbm, fo, in_sem.at[0])
     load_wt = pltpu.make_async_copy(wt_hbm, wt, in_sem.at[1])
-    load_leg = pltpu.make_async_copy(leg_hbm, leg, in_sem.at[2])
+    load_leg = pltpu.make_async_copy(leg_hbm, leg.at[0], in_sem.at[2])
     load_fo.start()
     load_wt.start()
     load_leg.start()
@@ -131,6 +131,13 @@
     def _():
         stay.start()
 
+    def to_sibling(src, dst, n):
+        return pltpu.make_async_remote_copy(
+            src_ref=src, dst_ref=dst, send_sem=x_send.at[n], recv_sem=x_recv.at[n],
+            device_id=(lat + step, wave), device_id_type=MESH)
+
+    give_leg = to_sibling(leg_hbm, leg.at[1], 0)
+    give_leg.start()
     load_leg.wait()
 
     def arrive(s, carry):
@@ -141,24 +148,35 @@
 
     north = ns[0:16].astype(F32)
     southern = ns[16:32].astype(F32)
-    eo[0] = (north + southern).astype(BF16).astype(F32).reshape(128, 128)
-    eo[1] = (north - southern).astype(BF16).astype(F32).reshape(128, 128)
+    both[0, 0] = (north + southern).astype(BF16).reshape(128, 128)
+    both[0, 1] = (north - southern).astype(BF16).reshape(128, 128)
+    give_both = to_sibling(both.at[0], both.at[1], 1)
+    give_both.start()
     sub = lax.broadcasted_iota(I32, (8, 128), 0)
     keep = [sub == 4 * kt + lane8 // 32 for kt in range(2)]
-    for part_of in range(2):
-        for pair in range(2):
-            turned = []
-            for c4 in (2 * pair, 2 * pair + 1):
-                x = eo[part_of, pl.ds(c4, 32, stride=4), :]
-                turned.append(jnp.concatenate([x] * 4, axis=0).T)
-            for g in range(3):
-                c = 4 * g + 2 * pair
-                for q in range(GROUPS):
-                    at = 40 * g + 8 * q
-                    for kt in range(2):
-                        both = jnp.concatenate(
-                            [jnp.where(keep[kt], t[at:at + 8], 0.0) for t in turned], axis=0)
-                        lhs[part_of, q, 8 * c:8 * c + 16, 128 * kt:128 * kt + 128] = both.astype(BF16)
+
+    def left_sides(source):
+        eo[...] = both[source].astype(F32)
+        for part_of in range(2):
+            for pair in range(2):
+                turned = []
+                for c4 in (2 * pair, 2 * pair + 1):
+                    x = eo[part_of, pl.ds(c4, 32, stride=4), :]
+                    turned.append(jnp.concatenate([x] * 4, axis=0).T)
+                for g in range(3):
+                    c = 4 * g + 2 * pair
+                    for q in range(GROUPS):
+                        at = 40 * g + 8 * q
+                        for kt in range(2):
+                            two_c = jnp.concatenate(
+                                [jnp.where(keep[kt], t[at:at + 8], 0.0) for t in turned], axis=0)
+                            lhs[source, part_of, q, 8 * c:8 * c + 16,
+                                128 * kt:128 * kt + 128] = two_c.astype(BF16)
+
+    left_sides(0)
+    give_both.wait_recv()
+    left_sides(1)
+    give_leg.wait_recv()
 
     lane96 = lanes((96, 128))
 
@@ -167,8 +185,11 @@
         column = pl.multiple_of(128 * ((5 * owner) // 4), 128)
         placed = [[], []]
         for q in range(GROUPS):
-            right = leg[8 * q:8 * q + 8, :, pl.ds(column, 256)].reshape(256, 256)
-            got = jnp.dot(lhs[owner // 4, q], right, preferred_element_type=F32)
+            got = sum(
+                jnp.dot(lhs[source, owner // 4, q],
+                        leg[source, 8 * q:8 * q + 8, :, pl.ds(column, 256)].reshape(256, 256),
+                        preferred_element_type=F32)
+                for source in range(2))
             for e in range(2):
                 start = off + OWN * e
                 window = jnp.where(lane96 >= start, got[:, :128], got[:, 128:])
@@ -185,11 +206,6 @@
                     rest = jnp.where(lane8 // 16 == n, pltpu.roll(z[4][8 * c:8 * c + 8], 16 * n, 1), rest)
                 part[job, e, 288 + 8 * v:296 + 8 * v] = rest
 
-    def to_sibling(job, e, slot):
-        return pltpu.make_async_remote_copy(
-            src_ref=part.at[job, e], dst_ref=sib.at[slot], send_sem=s_send.at[slot],
-            recv_sem=s_recv.at[slot], device_id=(lat + step, wave), device_id_type=MESH)
-
     def ring(slot, piece, at_lat, to_slot):
         low, high = PIECES[piece]
         return pltpu.make_async_remote_copy(
@@ -197,9 +213,9 @@
             send_sem=r_send.at[slot, piece], recv_sem=r_recv.at[to_slot, piece],
             device_id=(at_lat, wave), device_id_type=MESH)
 
-    def pass_on(slot, job, e, from_sib, arrived, at_lat, to_slot):
+    def pass_on(slot, job, e, arrived, at_lat, to_slot):
         for piece, (low, high) in enumerate(PIECES):
-            total = part[job, e, low:high] + sib[from_sib, low:high]
+            total = part[job, e, low:high]
             for had in arrived:
                 ring(0, piece, at_lat, had).wait_recv()
                 total = total + rrcv[had, low:high].astype(F32)
@@ -210,59 +226,38 @@
     other = 1 - core
 
     def work(job, carry):
-        toward = job % 2 == 0
-        far = jnp.where(job == 0, 4, jnp.where(job == 7, 0, 3 - (job - 1) // 2))
-        owner = chip_at(jnp.where(toward, far, -far))
-        product(job, owner)
+        distance = jnp.where(job < 2, 3 + job, jnp.where(job < 4, job - 1, 0))
+        product(job, chip_at(distance))
 
         @pl.when(job == 0)
         def _():
-            to_sibling(0, other, 0).start()
-
-        for k in (1, 3, 5):
-            @pl.when(job == k)
-            def _():
-                to_sibling(k, 0, k).start()
-                to_sibling(k, 1, k + 1).start()
-
-        @pl.when(job == 7)
+            pass_on(1 + other, 0, other, (), one + core, 1 + other)
+            pass_on(1 + core, 0, core, (), one + core, 1 + core)
+
+        @pl.when(job == 1)
         def _():
-            to_sibling(7, other, 7).start()
+            pass_on(0, 1, core, (), two + core, 0)
 
         @pl.when(job == 2)
         def _():
-            to_sibling(0, other, 0).wait_recv()
-            pass_on(0, 0, core, 0, (), two + core, 0)
-            to_sibling(1, 0, 1).wait_recv()
-            pass_on(1, 2, 0, 1, (), one + core, 1)
-            to_sibling(1, 1, 2).wait_recv()
-            pass_on(2, 2, 1, 2, (), one + core, 2)
-
-        @pl.when(job == 6)
+            pass_on(3, 2, 0, (), one, 3 + core)
+            pass_on(4, 2, 1, (), one + 1, 3 + core)
+
+        @pl.when(job == 4)
         def _():
-            to_sibling(5, 0, 5).wait_recv()
-            pass_on(3, 6, 0, 5, (), one, 3 + core)
-            to_sibling(5, 1, 6).wait_recv()
-            pass_on(4, 6, 1, 6, (), one + 1, 3 + core)
-
-        @pl.when(job == 7)
-        def _():
-            to_sibling(3, 0, 3).wait_recv()
-            to_sibling(3, 1, 4).wait_recv()
-            pass_on(5 + other, 4, other, 3 + other, (1 + other,), two + other, 5 + core)
-            pass_on(5 + core, 4, core, 3 + core, (1 + core, 0), two + core, 5 + core)
-
-        return carry
-
-    lax.fori_loop(0, 8, work, 0)
-
-    to_sibling(7, other, 7).wait_recv()
+            pass_on(5 + other, 3, other, (1 + other,), two + other, 5 + core)
+            pass_on(5 + core, 3, core, (1 + core, 0), two + core, 5 + core)
+
+        return carry
+
+    lax.fori_loop(0, 5, work, 0)
+
     for slot in range(3, 7):
         for piece in range(len(PIECES)):
             ring(0, piece, one, slot).wait_recv()
 
     def total(low, high):
-        return (part[7, core, low:high] + sib[7, low:high]
+        return (part[4, core, low:high]
                 + rrcv[3, low:high].astype(F32) + rrcv[4, low:high].astype(F32)
                 + rrcv[5, low:high].astype(F32) + rrcv[6, low:high].astype(F32))
 
@@ -294,8 +289,8 @@
     def _():
         exchange(WAVES - 1).wait_send()
 
-    for slot in range(8):
-        to_sibling(0, 0, slot).wait_send()
+    give_leg.wait_send()
+    give_both.wait_send()
     for slot in range(7):
         for piece in range(len(PIECES)):
             ring(slot, piece, one, 0).wait_send()
@@ -312,22 +307,22 @@
         scratch_shapes=[
             pltpu.VMEM((COLS, 2, DEG), BF16),
             pltpu.VMEM((10, 128), I32),
-            pltpu.VMEM((SLOTS, PAIRS, DEG), BF16),
+            pltpu.VMEM((2, SLOTS, PAIRS, DEG), BF16),
             pltpu.VMEM((3, 8, DEG), F32),
             pltpu.VMEM((33, 8, 128), BF16),
             pltpu.VMEM((32, 8, 128), BF16),
             pltpu.VMEM((2, 128, 128), F32),
-            pltpu.VMEM((2, GROUPS, 96, 256), BF16),
+            pltpu.VMEM((2, 2, 128, 128), BF16),
+            pltpu.VMEM((2, 2, GROUPS, 96, 256), BF16),
             pltpu.VMEM((SLOTS, 128), F32),
-            pltpu.VMEM((8, 2, ROWS, 128), F32),
-            pltpu.VMEM((8, ROWS, 128), F32),
+            pltpu.VMEM((5, 2, ROWS, 128), F32),
             pltpu.VMEM((7, ROWS, 128), BF16),
             pltpu.VMEM((7, ROWS, 128), BF16),
             pltpu.SemaphoreType.DMA((3,)),
             pltpu.SemaphoreType.DMA((WAVES,)),
             pltpu.SemaphoreType.DMA((WAVES,)),
-            pltpu.SemaphoreType.DMA((8,)),
-            pltpu.SemaphoreType.DMA((8,)),
+            pltpu.SemaphoreType.DMA((2,)),
+            pltpu.SemaphoreType.DMA((2,)),
             pltpu.SemaphoreType.DMA((7, len(PIECES))),
             pltpu.SemaphoreType.DMA((7, len(PIECES))),
         ],

time: 39.6 us -> 38.4 us (0.970)
  Pallas kernels: 38.8 us -> 37.6 us
    pallas_call x1, Pallas kernels: 38.8 us -> 37.6 us  [local(): pl.pallas_call(kernel, out_shape=jax.ShapeDtypeStruct((COLS, SLOTS, OWN),...]
where the time goes in v4:
time: 38.4 us; the launch traced here: 38.3 us
  Pallas kernels  37.6 us (98%)
  local copies, waits for them, and re-layouts  0.7 us (2%)
    pallas_call x1, Pallas kernels, local(): pl.pallas_call(kernel, out_shape=jax.ShapeDtypeStruct((COLS, SLOTS, OWN),...  37.6 us

profile of v4, /device:TPU:8, one launch (start us, length us, event | category | flops | bytes accessed | tf_op | source)
XLA Modules:
  0.0 38.3 jit_solution(3428351267559996855)
XLA Ops:
  0.0 37.6 %legendre.1 = f32[12,40,80]{2,1,0:T(8,128)S(1)} custom-call(bf16[12,2,1280]{2,1,0:T(2,128)(2,1)} %bitcast.4, s32[10,128]{1,0:T(8,128)} %bitcast.5, bf16[40,32,1280]{2,1,0:T(8,128)(2,1)} %leg_hbm.1), custom_call_target="tpu_custom_call" | custom-call | tf_op jit(solution)/shard_map/legendre/pallas_call | solution.py:302
  37.6 0.7 %copy.5 = f32[40,12,80]{2,0,1:T(8,128)} copy(f32[40,12,80]{2,0,1:T(8,128)S(1)} %bitcast.3) | data formatting | bytes 307200

commit v5 on v4

--- a/solution.py
+++ b/solution.py
@@ -226,17 +226,17 @@
     other = 1 - core
 
     def work(job, carry):
-        distance = jnp.where(job < 2, 3 + job, jnp.where(job < 4, job - 1, 0))
+        distance = jnp.where(job < 2, 4 - job, jnp.where(job < 4, job - 1, 0))
         product(job, chip_at(distance))
 
         @pl.when(job == 0)
         def _():
-            pass_on(1 + other, 0, other, (), one + core, 1 + other)
-            pass_on(1 + core, 0, core, (), one + core, 1 + core)
+            pass_on(0, 0, core, (), two + core, 0)
 
         @pl.when(job == 1)
         def _():
-            pass_on(0, 1, core, (), two + core, 0)
+            pass_on(1 + other, 1, other, (), one + core, 1 + other)
+            pass_on(1 + core, 1, core, (), one + core, 1 + core)
 
         @pl.when(job == 2)
         def _():
@@ -252,13 +252,18 @@
 
     lax.fori_loop(0, 5, work, 0)
 
-    for slot in range(3, 7):
+    def landed(slot):
         for piece in range(len(PIECES)):
             ring(0, piece, one, slot).wait_recv()
 
+    landed(3)
+    landed(4)
+    part[4, core] += rrcv[3].astype(F32) + rrcv[4].astype(F32)
+    landed(5)
+    landed(6)
+
     def total(low, high):
         return (part[4, core, low:high]
-                + rrcv[3, low:high].astype(F32) + rrcv[4, low:high].astype(F32)
                 + rrcv[5, low:high].astype(F32) + rrcv[6, low:high].astype(F32))
 
     t0, t1, t2, rest = total(0, 96), total(96, 192), total(192, 288), total(288, 304)

time: 38.4 us -> 38.3 us (level)
  no operation moved by 1% of the time
where the time goes in v5:
time: 38.3 us; the launch traced here: 38.1 us
  Pallas kernels  37.4 us (98%)
  local copies, waits for them, and re-layouts  0.7 us (2%)
    pallas_call x1, Pallas kernels, local(): pl.pallas_call(kernel, out_shape=jax.ShapeDtypeStruct((COLS, SLOTS, OWN),...  37.4 us

profile of v5, /device:TPU:8, one launch (start us, length us, event | category | flops | bytes accessed | tf_op | source)
XLA Modules:
  0.0 38.1 jit_solution(10344522174504741498)
XLA Ops:
  0.0 37.4 %legendre.1 = f32[12,40,80]{2,1,0:T(8,128)S(1)} custom-call(bf16[12,2,1280]{2,1,0:T(2,128)(2,1)} %bitcast.4, s32[10,128]{1,0:T(8,128)} %bitcast.5, bf16[40,32,1280]{2,1,0:T(8,128)(2,1)} %leg_hbm.1), custom_call_target="tpu_custom_call" | custom-call | tf_op jit(solution)/shard_map/legendre/pallas_call | solution.py:307
  37.4 0.7 %copy.5 = f32[40,12,80]{2,0,1:T(8,128)} copy(f32[40,12,80]{2,0,1:T(8,128)S(1)} %bitcast.3) | data formatting | bytes 307200

commit v6 on v5

--- a/solution.py
+++ b/solution.py
@@ -13,7 +13,7 @@
 OWN = 80
 ROWS = 304
 GROUPS = 5
-PIECES = ((0, 160), (160, 304))
+PIECES = ((0, 112), (112, 208), (208, 304))
 
 
 def lanes(shape):

time: 38.3 us -> 38.1 us (level)
  no operation moved by 1% of the time
where the time goes in v6:
time: 38.1 us; the launch traced here: 38 us
  Pallas kernels  37.3 us (98%)
  local copies, waits for them, and re-layouts  0.7 us (2%)
    pallas_call x1, Pallas kernels, local(): pl.pallas_call(kernel, out_shape=jax.ShapeDtypeStruct((COLS, SLOTS, OWN),...  37.3 us

profile of v6, /device:TPU:8, one launch (start us, length us, event | category | flops | bytes accessed | tf_op | source)
XLA Modules:
  0.0 38.0 jit_solution(9656139965716714354)
XLA Ops:
  0.0 37.3 %legendre.1 = f32[12,40,80]{2,1,0:T(8,128)S(1)} custom-call(bf16[12,2,1280]{2,1,0:T(2,128)(2,1)} %bitcast.4, s32[10,128]{1,0:T(8,128)} %bitcast.5, bf16[40,32,1280]{2,1,0:T(8,128)(2,1)} %leg_hbm.1), custom_call_target="tpu_custom_call" | custom-call | tf_op jit(solution)/shard_map/legendre/pallas_call | solution.py:307
  37.3 0.7 %copy.5 = f32[40,12,80]{2,0,1:T(8,128)} copy(f32[40,12,80]{2,0,1:T(8,128)S(1)} %bitcast.3) | data formatting | bytes 307200
